TPU v7x, 32 devices: a whole 2x2x4 slice. The times are simulated.
32 devices in a mesh: job: 2 (over y), chain: 4 (over z), pair: 2 (over x), pno: 2 (over core).
Axes of the slice: x: 2, y: 2, z: 4, core: 2. Of those that a mesh axis runs over, the one named last changes fastest.
Arguments:
- amplitudes: bfloat16 [96, 128, 128], P(('job', 'chain', 'pair'), 'pno'), parts along dimension 0, may hold values from -4 to 4
- integrals: bfloat16 [96, 128, 128], P(('job', 'chain', 'pair'), 'pno'), parts along dimension 0, may hold values from -6 to 6
- intersections: bfloat16 [96, 32, 128, 128], P(('job', 'chain', 'pair')), parts along dimension 0, may hold values from -0.5 to 0.5
- coupling: float32 [96, 32], P(('job', 'chain', 'pair')), parts along dimension 0, may hold values from -4 to 4
- pno_energies: float32 [96, 128], P(('job', 'chain', 'pair')), parts along dimension 0, may hold values from 0.3 to 3
- pair_shift: float32 [96], P(('job', 'chain', 'pair')), parts along dimension 0, may hold values from -1.5 to -0.3
- ranks: int32 [96], P(('job', 'chain', 'pair')), parts along dimension 0, may hold values from 24 to 128
- neighbours: int32 [96, 32], P(('job', 'chain', 'pair')), parts along dimension 0, may hold values from 0 to 47, as said below
Outputs:
- final_amplitudes: bfloat16 [96, 128, 128], P(('job', 'chain', 'pair'), 'pno'), parts along dimension 0
- residual_norms: float32 [6], P('job'), parts along dimension 0
There are 2 independent parts, one for each index of `job`. A program takes and returns all parts, laid end to end along the dimension named above; each array names one. Nothing has to cross between parts.
Inputs may be any that keep to these rules, and one draw needn't show every extreme that they name: `neighbours`: every coupled pair of pair g lies in the fragment of g (pairs k * 12 to (k + 1) * 12 - 1 for k = g // 12) or in one of the two fragments beside it.
All inputs are finite; a program needn't handle non-finite values.
Results may differ from a plain program's by a relative error of at most 0.015.
Values may be sent and summed in bfloat16 or wider, within the bound.
A program may use at most 64 MiB of HBM per device.

v0:
```python
import jax
import jax.numpy as jnp
from jax import lax
from jax.sharding import PartitionSpec as P

ITERS = 3


def padded(cells, sides, width):
    for axis, dim in sides:
        count = lax.axis_size(axis)
        ends = count - 1
        head = lax.slice_in_dim(cells, 0, width, axis=dim)
        tail = lax.slice_in_dim(cells, cells.shape[dim] - width, cells.shape[dim], axis=dim)
        cells = jnp.concatenate(
            [
                lax.ppermute(tail, axis, [(i, (i + 1) % count) for i in range(ends)]),
                cells,
                lax.ppermute(head, axis, [((i + 1) % count, i) for i in range(ends)]),
            ],
            axis=dim,
        )
    return cells


def spread_amps(piece):
    whole_rows = lax.all_gather(piece, "pno", axis=1, tiled=True)
    fragment_set = lax.all_gather(whole_rows, "pair", axis=0, tiled=True)
    return padded(fragment_set, (("chain", 0),), fragment_set.shape[0])


def spread_delta(piece):
    whole_rows = lax.all_gather(piece.astype(jnp.bfloat16), "pno", axis=1, tiled=True).astype(
        piece.dtype
    )
    fragment_set = lax.all_gather(
        whole_rows.astype(jnp.bfloat16), "pair", axis=0, tiled=True
    ).astype(whole_rows.dtype)
    return padded(fragment_set.astype(jnp.bfloat16), (("chain", 0),), fragment_set.shape[0]).astype(
        fragment_set.dtype
    )


def per_device(
    amplitudes, integrals, intersections, coupling, pno_energies, pair_shift, ranks, neighbours
):
    count = amplitudes.shape[0]
    half = amplitudes.shape[1]
    width = amplitudes.shape[2]
    chain_pos = lax.axis_index("chain")
    first_row = lax.axis_index("pno") * half
    frag = count * lax.axis_size("pair")
    cells = frag * lax.axis_size("chain") * width * width
    columns = jnp.arange(width, dtype=jnp.int32)
    rows_here = first_row + jnp.arange(half, dtype=jnp.int32)
    live_cols = columns[None, :] < ranks[:, None]
    live_rows = rows_here[None, :] < ranks[:, None]
    mask = (live_rows[:, :, None] & live_cols[:, None, :]).astype(jnp.float32)
    energy_rows = lax.dynamic_slice_in_dim(pno_energies, first_row, half, 1)
    denom = energy_rows[:, :, None] + pno_energies[:, None, :] - pair_shift[:, None, None]
    over_rows = lax.dynamic_slice_in_dim(intersections, first_row, half, 2)
    own = (amplitudes.astype(jnp.float32) * mask).astype(jnp.bfloat16)
    ints = integrals.astype(jnp.float32)
    slots = neighbours - (chain_pos - 1) * frag
    window = spread_amps(own)
    norms = []
    for step_no in range(ITERS):
        blocks = jnp.take(window, slots, axis=0)
        proj = jnp.einsum(
            "pnab,pnbc->pnac", over_rows, blocks, preferred_element_type=jnp.float32
        ).astype(jnp.bfloat16)
        terms = jnp.einsum(
            "pnac,pnbc->pnab", proj, intersections, preferred_element_type=jnp.float32
        )
        coupled = jnp.einsum("pn,pnab->pab", coupling, terms)
        own32 = own.astype(jnp.float32)
        resid = mask * (ints + coupled - denom * own32)
        delta = resid / denom
        more = step_no + 1 < ITERS
        if more:
            moved = spread_delta(delta)
        squares = lax.psum(jnp.sum(resid * resid), ("chain", "pair", "pno"))
        rms = jnp.sqrt(squares / cells)
        factor = 1.0 / (1.0 + rms)
        norms.append(rms)
        own = (own32 + delta * factor).astype(jnp.bfloat16)
        if more:
            window = (window.astype(jnp.float32) + moved * factor).astype(jnp.bfloat16)
    return (own, jnp.stack(norms))


def solution(mesh):
    in_specs = (
        P(("job", "chain", "pair"), "pno", None),
        P(("job", "chain", "pair"), "pno", None),
        P(("job", "chain", "pair"), None, None, None),
        P(("job", "chain", "pair"), None),
        P(("job", "chain", "pair"), None),
        P(("job", "chain", "pair")),
        P(("job", "chain", "pair")),
        P(("job", "chain", "pair"), None),
    )
    out_specs = (P(("job", "chain", "pair"), "pno", None), P("job"))
    return jax.shard_map(
        per_device, mesh=mesh, in_specs=in_specs, out_specs=out_specs, check_vma=False
    )
```

profile of v0, /device:TPU:0, one launch (start us, length us, event | category | flops | bytes accessed | tf_op | source)
XLA Modules:
  0.0 237.0 jit_solution(1108903351349662818)
XLA Ops:
  0.6 0.0 copy-start
  0.7 0.7 iota_compare_fusion
  1.4 0.0 copy-start.6
  1.4 0.7 broadcast_compare_fusion
  2.1 0.0 copy-start.4
  2.1 1.0 fusion.48
  3.1 2.1 all_gather.18
  5.2 8.7 %all_gather.19 = bf16[12,128,128]{2,1,0:T(8,128)(2,1)S(1)} all-gather(bf16[6,128,128]{2,1,0:T(8,128)(2,1)S(1)} %all_gather.18), channel_id=1, replica_groups=mesh['job'=2,'chain'=4,'pair'=2,'pno'=2] {'pair'}, dimensions={0}, use_global_device_ids=true | all-gather | bytes 589824 | tf_op jit(solution)/shard_map/all_gather | solution.py:28
  13.9 1.3 collective-permute-start.1
  15.2 4.6 %collective-permute-start = (bf16[12,128,128]{2,1,0:T(8,128)(2,1)S(1)}, bf16[12,128,128]{2,1,0:T(8,128)(2,1)S(1)}, u32[]{:S(2)}, u32[]{:S(2)}) collective-permute-start(bf16[12,128,128]{2,1,0:T(8,128)(2,1)S(1)} %all_gather.19), channel_id=1, source_target_pairs={{0,4},{4,8},{8,12},{1,5},{5,9},{9,13},{2,6},{6,10},{10,14},{3,7},{... | collective-permute-start | bytes 1179656 | tf_op jit(solution)/shard_map/ppermute | solution.py:17
  19.8 0.7 compare_and_fusion
  20.5 0.1 reshape.89
  20.6 0.8 constant_dynamic-slice_fusion
  21.3 6.2 %collective-permute-done = bf16[12,128,128]{2,1,0:T(8,128)(2,1)S(1)} collective-permute-done((bf16[12,128,128]{2,1,0:T(8,128)(2,1)S(1)}, bf16[12,128,128]{2,1,0:T(8,128)(2,1)S(1)}, u32[]{:S(2)}, u32[]{:S(2)}) %collective-permute-start) | collective-permute-done | bytes 393248 | tf_op jit(solution)/shard_map/ppermute | solution.py:17
  27.6 0.1 constant_dynamic-update-slice_fusion.1
  27.7 0.0 collective-permute-done.1
  27.7 0.1 constant_dynamic-update-slice_fusion
  27.7 8.0 %gather_fusion = bf16[192,128,128]{2,1,0:T(8,128)(2,1)} fusion(bf16[36,128,128]{2,1,0:T(8,128)(2,1)S(1)} %constant_dynamic-update-slice_fusion, s32[1024]{0:T(1024)S(1)} %pad_clamp_fusion), kind=kCustom, calls=%fused_computation.clone | custom fusion | bytes 12583680 | tf_op jit(solution)/shard_map/jit(_take)/gather | solution.py:68
  35.7 10.8 %fusion.22 = bf16[6,32,64,128]{3,2,1,0:T(8,128)(2,1)} fusion(bf16[6,32,128,128]{3,2,1,0:T(8,128)(2,1)} %param.12, bf16[6,32,128,128]{3,2,1,0:T(8,128)(2,1)} %bitcast.20, pred[6,32]{1,0:T(8,128)(4,1)S(1)} %get-tuple-element.5, s32[]{:T(128)S(6)} %select_n.11), kind=kOutput, calls=%fused_computation.25 | convolution fusion | flops 810024960 | bytes 18874564 | tf_op jit(solution)/shard_map/pnac,pnbc->pnab/dot_general | solution.py:72
  46.5 0.0 copy-done
  46.6 0.0 copy-start.3
  46.6 0.0 copy-start.8
  46.6 3.8 %fusion.4 = f32[6,1,64,128]{3,1,2,0:T(1,128)S(1)} fusion(bf16[6,32,64,128]{3,2,1,0:T(8,128)(2,1)} %fusion.22, f32[6,32,1,1]{1,0,2,3:T(8,128)S(1)} %bitcast.16), kind=kOutput, calls=%fused_computation.7 | convolution fusion | flops 3145728 | bytes 3343104 | tf_op jit(solution)/shard_map/pn,pnab->pab/dot_general | solution.py:75
  50.4 0.0 copy-done.1
  50.4 0.0 copy-done.2
  50.4 0.0 copy-done.3
  50.4 0.0 copy-done.8
  50.4 0.8 multiply_reduce_fusion.2
  51.2 1.9 all_gather.20
  53.1 7.6 %all_gather.21 = bf16[12,128,128]{2,1,0:T(8,128)(2,1)S(1)} all-gather(bf16[6,128,128]{2,1,0:T(8,128)(2,1)S(1)} %all_gather.20), channel_id=1, replica_groups=mesh['job'=2,'chain'=4,'pair'=2,'pno'=2] {'pair'}, dimensions={0}, use_global_device_ids=true | all-gather | bytes 589824 | tf_op jit(solution)/shard_map/all_gather | solution.py:36
  60.7 1.3 collective-permute-start.3
  62.0 5.8 %collective-permute-start.2 = (bf16[12,128,128]{2,1,0:T(8,128)(2,1)S(1)}, bf16[12,128,128]{2,1,0:T(8,128)(2,1)}, u32[]{:S(2)}, u32[]{:S(2)}) collective-permute-start(bf16[12,128,128]{2,1,0:T(8,128)(2,1)S(1)} %all_gather.21), channel_id=1, source_target_pairs={{0,4},{4,8},{8,12},{1,5},{5,9},{9,13},{2,6},{6,10},{10,14},{3,7},{... | collective-permute-start | bytes 1179656 | tf_op jit(solution)/shard_map/ppermute | solution.py:17
  67.8 34.8 %psum.21 = f32[]{:T(128)} all-reduce(f32[]{:T(128)} %get-tuple-element.7), channel_id=1, replica_groups=mesh['job'=2,'chain'=4,'pair'=2,'pno'=2] {'chain','pair','pno'}, use_global_device_ids=true, to_apply=%region_1.3 | all-reduce | flops 1 | bytes 8 | tf_op jit(solution)/shard_map/psum | solution.py:82
  103.3 0.0 collective-permute-done.3
  103.3 0.0 collective-permute-done.2
  103.3 1.6 add_convert_fusion.1
  104.9 8.0 %gather_fusion.1 = bf16[192,128,128]{2,1,0:T(8,128)(2,1)} fusion(bf16[36,128,128]{2,1,0:T(8,128)(2,1)S(1)} %add_convert_fusion.1, s32[1024]{0:T(1024)S(1)} %pad_clamp_fusion), kind=kCustom, calls=%fused_computation.1.clone | custom fusion | bytes 12583680 | tf_op jit(solution)/shard_map/jit(_take)/gather | solution.py:68
  112.9 0.0 copy-done.10
  112.9 10.8 %fusion.20 = bf16[6,32,64,128]{3,2,1,0:T(8,128)(2,1)} fusion(bf16[6,32,128,128]{3,2,1,0:T(8,128)(2,1)} %param.12, bf16[6,32,128,128]{3,2,1,0:T(8,128)(2,1)} %bitcast.21, pred[6,32]{1,0:T(8,128)(4,1)S(1)} %get-tuple-element.5, s32[]{:T(128)S(6)} %select_n.11), kind=kOutput, calls=%fused_computation.23 | convolution fusion | flops 810024960 | bytes 18874564 | tf_op jit(solution)/shard_map/pnac,pnbc->pnab/dot_general | solution.py:72
  123.7 3.7 %fusion.2 = f32[6,1,64,128]{3,1,2,0:T(1,128)S(1)} fusion(bf16[6,32,64,128]{3,2,1,0:T(8,128)(2,1)} %fusion.20, f32[6,32,1,1]{1,0,2,3:T(8,128)S(1)} %bitcast.18), kind=kOutput, calls=%fused_computation.5 | convolution fusion | flops 3145728 | bytes 3343104 | tf_op jit(solution)/shard_map/pn,pnab->pab/dot_general | solution.py:75
  127.5 0.8 multiply_reduce_fusion.1
  128.3 0.0 copy-done.6
  128.3 0.0 copy-done.4
  128.3 0.2 fusion.52
  128.5 1.9 all_gather.22
  130.4 7.6 %all_gather.23 = bf16[12,128,128]{2,1,0:T(8,128)(2,1)S(1)} all-gather(bf16[6,128,128]{2,1,0:T(8,128)(2,1)S(1)} %all_gather.22), channel_id=1, replica_groups=mesh['job'=2,'chain'=4,'pair'=2,'pno'=2] {'pair'}, dimensions={0}, use_global_device_ids=true | all-gather | bytes 589824 | tf_op jit(solution)/shard_map/all_gather | solution.py:36
  138.0 1.3 collective-permute-start.5
  139.3 5.3 %collective-permute-start.4 = (bf16[12,128,128]{2,1,0:T(8,128)(2,1)S(1)}, bf16[12,128,128]{2,1,0:T(8,128)(2,1)}, u32[]{:S(2)}, u32[]{:S(2)}) collective-permute-start(bf16[12,128,128]{2,1,0:T(8,128)(2,1)S(1)} %all_gather.23), channel_id=1, source_target_pairs={{0,4},{4,8},{8,12},{1,5},{5,9},{9,13},{2,6},{6,10},{10,14},{3,7},{... | collective-permute-start | bytes 1179656 | tf_op jit(solution)/shard_map/ppermute | solution.py:17
  144.6 34.4 %psum.22 = f32[]{:T(128)} all-reduce(f32[]{:T(128)} %get-tuple-element.3), channel_id=1, replica_groups=mesh['job'=2,'chain'=4,'pair'=2,'pno'=2] {'chain','pair','pno'}, use_global_device_ids=true, to_apply=%region_3.5 | all-reduce | flops 1 | bytes 8 | tf_op jit(solution)/shard_map/psum | solution.py:82
  179.7 0.0 collective-permute-done.5
  179.7 0.0 collective-permute-done.4
  179.7 1.5 add_convert_fusion
  181.3 0.0 copy-start.11
  181.3 8.0 %gather_fusion.2 = bf16[192,128,128]{2,1,0:T(8,128)(2,1)} fusion(bf16[36,128,128]{2,1,0:T(8,128)(2,1)S(1)} %add_convert_fusion, s32[1024]{0:T(1024)S(1)} %pad_clamp_fusion), kind=kCustom, calls=%fused_computation.2.clone | custom fusion | bytes 12583680 | tf_op jit(solution)/shard_map/jit(_take)/gather | solution.py:68
  189.3 0.0 copy-done.11
  189.3 10.8 %fusion.18 = bf16[6,32,64,128]{3,2,1,0:T(8,128)(2,1)} fusion(bf16[6,32,128,128]{3,2,1,0:T(8,128)(2,1)} %param.12, bf16[6,32,128,128]{3,2,1,0:T(8,128)(2,1)} %bitcast.19, pred[6,32]{1,0:T(8,128)(4,1)S(1)} %copy-done.11, s32[]{:T(128)S(6)} %select_n.11), kind=kOutput, calls=%fused_computation.21 | convolution fusion | flops 810024960 | bytes 18874564 | tf_op jit(solution)/shard_map/pnac,pnbc->pnab/dot_general | solution.py:72
  200.1 3.7 %fusion = f32[6,1,64,128]{3,1,2,0:T(1,128)S(1)} fusion(bf16[6,32,64,128]{3,2,1,0:T(8,128)(2,1)} %fusion.18, f32[6,32,1,1]{1,0,2,3:T(8,128)S(1)} %bitcast.17), kind=kOutput, calls=%fused_computation.3 | convolution fusion | flops 3145728 | bytes 3343104 | tf_op jit(solution)/shard_map/pn,pnab->pab/dot_general | solution.py:75
  203.8 0.0 copy-done.5
  203.8 0.0 copy-done.7
  203.9 0.0 copy-done.9
  203.9 0.8 multiply_reduce_fusion
  204.7 30.1 %psum.23 = f32[]{:T(128)} all-reduce(f32[]{:T(128)} %multiply_reduce_fusion), channel_id=1, replica_groups=mesh['job'=2,'chain'=4,'pair'=2,'pno'=2] {'chain','pair','pno'}, use_global_device_ids=true, to_apply=%region_5.7 | all-reduce | flops 1 | bytes 8 | tf_op jit(solution)/shard_map/psum | solution.py:82
  235.5 0.9 fusion.47
  236.4 0.6 pad_maximum_fusion
  (9 shorter events, 0.0 us)
Async XLA Ops:
  0.6 45.9 %copy-start = (f32[6,32]{1,0:T(8,128)S(1)}, f32[6,32]{1,0:T(8,128)}, u32[]{:S(2)}) copy-start(f32[6,32]{1,0:T(8,128)} %param.13) | copy-start | bytes 2308
  1.4 126.9 %copy-start.6 = (pred[6,128]{1,0:T(8,128)(4,1)}, pred[6,128]{1,0:T(8,128)(4,1)S(1)}, u32[]{:S(2)}) copy-start(pred[6,128]{1,0:T(8,128)(4,1)S(1)} %iota_compare_fusion) | copy-start | bytes 2308
  2.1 126.2 %copy-start.4 = (pred[6,64]{1,0:T(8,128)(4,1)}, pred[6,64]{1,0:T(8,128)(4,1)S(1)}, u32[]{:S(2)}) copy-start(pred[6,64]{1,0:T(8,128)(4,1)S(1)} %broadcast_compare_fusion) | copy-start | bytes 1156
  13.9 13.7 %collective-permute-start.1 = (bf16[12,128,128]{2,1,0:T(8,128)(2,1)S(1)}, bf16[12,128,128]{2,1,0:T(8,128)(2,1)S(1)}, u32[]{:S(2)}, u32[]{:S(2)}) collective-permute-start(bf16[12,128,128]{2,1,0:T(8,128)(2,1)S(1)} %all_gather.19), channel_id=1, source_target_pairs={{4,0},{8,4},{12,8},{5,1},{9,5},{13,9},{6,2},{10,6},{14,10},{7,3},{... | collective-permute-start | bytes 1179656 | tf_op jit(solution)/shard_map/ppermute | solution.py:19
  15.2 12.4 %collective-permute-start = (bf16[12,128,128]{2,1,0:T(8,128)(2,1)S(1)}, bf16[12,128,128]{2,1,0:T(8,128)(2,1)S(1)}, u32[]{:S(2)}, u32[]{:S(2)}) collective-permute-start(bf16[12,128,128]{2,1,0:T(8,128)(2,1)S(1)} %all_gather.19), channel_id=1, source_target_pairs={{0,4},{4,8},{8,12},{1,5},{5,9},{9,13},{2,6},{6,10},{10,14},{3,7},{... | collective-permute-start | bytes 1179656 | tf_op jit(solution)/shard_map/ppermute | solution.py:17
  20.5 92.4 %copy-start.10 = (pred[6,32]{1,0:T(8,128)(4,1)}, pred[6,32]{1,0:T(8,128)(4,1)S(1)}, u32[]{:S(2)}) copy-start(pred[6,32]{1,0:T(8,128)(4,1)S(1)} %get-tuple-element.5) | copy-start | bytes 580
  46.5 3.8 %copy-start.1 = (bf16[6,64,128]{2,1,0:T(8,128)(2,1)S(1)}, bf16[6,64,128]{2,1,0:T(8,128)(2,1)}, u32[]{:S(2)}) copy-start(bf16[6,64,128]{2,1,0:T(8,128)(2,1)} %param.11) | copy-start | bytes 294916
  46.6 3.8 %copy-start.2 = (bf16[6,64,128]{2,1,0:T(8,128)(2,1)S(1)}, bf16[6,64,128]{2,1,0:T(8,128)(2,1)}, u32[]{:S(2)}) copy-start(bf16[6,64,128]{2,1,0:T(8,128)(2,1)} %param.10) | copy-start | bytes 294916
  46.6 3.8 %copy-start.3 = (f32[6,128]{1,0:T(8,128)S(1)}, f32[6,128]{1,0:T(8,128)}, u32[]{:S(2)}) copy-start(f32[6,128]{1,0:T(8,128)} %param.14) | copy-start | bytes 9220
  46.6 3.8 %copy-start.8 = (f32[6]{0:T(128)S(1)}, f32[6]{0:T(128)}, u32[]{:S(2)}) copy-start(f32[6]{0:T(128)} %param.15) | copy-start | bytes 76
  60.7 42.6 %collective-permute-start.3 = (bf16[12,128,128]{2,1,0:T(8,128)(2,1)S(1)}, bf16[12,128,128]{2,1,0:T(8,128)(2,1)}, u32[]{:S(2)}, u32[]{:S(2)}) collective-permute-start(bf16[12,128,128]{2,1,0:T(8,128)(2,1)S(1)} %all_gather.21), channel_id=1, source_target_pairs={{4,0},{8,4},{12,8},{5,1},{9,5},{13,9},{6,2},{10,6},{14,10},{7,3},{... | collective-permute-start | bytes 1179656 | tf_op jit(solution)/shard_map/ppermute | solution.py:19
  62.0 41.3 %collective-permute-start.2 = (bf16[12,128,128]{2,1,0:T(8,128)(2,1)S(1)}, bf16[12,128,128]{2,1,0:T(8,128)(2,1)}, u32[]{:S(2)}, u32[]{:S(2)}) collective-permute-start(bf16[12,128,128]{2,1,0:T(8,128)(2,1)S(1)} %all_gather.21), channel_id=1, source_target_pairs={{0,4},{4,8},{8,12},{1,5},{5,9},{9,13},{2,6},{6,10},{10,14},{3,7},{... | collective-permute-start | bytes 1179656 | tf_op jit(solution)/shard_map/ppermute | solution.py:17
  138.0 41.7 %collective-permute-start.5 = (bf16[12,128,128]{2,1,0:T(8,128)(2,1)S(1)}, bf16[12,128,128]{2,1,0:T(8,128)(2,1)S(1)}, u32[]{:S(2)}, u32[]{:S(2)}) collective-permute-start(bf16[12,128,128]{2,1,0:T(8,128)(2,1)S(1)} %all_gather.23), channel_id=1, source_target_pairs={{4,0},{8,4},{12,8},{5,1},{9,5},{13,9},{6,2},{10,6},{14,10},{7,3},{... | collective-permute-start | bytes 1179656 | tf_op jit(solution)/shard_map/ppermute | solution.py:19
  139.3 40.4 %collective-permute-start.4 = (bf16[12,128,128]{2,1,0:T(8,128)(2,1)S(1)}, bf16[12,128,128]{2,1,0:T(8,128)(2,1)}, u32[]{:S(2)}, u32[]{:S(2)}) collective-permute-start(bf16[12,128,128]{2,1,0:T(8,128)(2,1)S(1)} %all_gather.23), channel_id=1, source_target_pairs={{0,4},{4,8},{8,12},{1,5},{5,9},{9,13},{2,6},{6,10},{10,14},{3,7},{... | collective-permute-start | bytes 1179656 | tf_op jit(solution)/shard_map/ppermute | solution.py:17
  181.3 8.0 %copy-start.11 = (pred[6,32]{1,0:T(8,128)(4,1)S(1)}, pred[6,32]{1,0:T(8,128)(4,1)}, u32[]{:S(2)}) copy-start(pred[6,32]{1,0:T(8,128)(4,1)} %copy-done.10) | copy-start | bytes 580
  200.1 3.8 %copy-start.5 = (pred[6,64]{1,0:T(8,128)(4,1)S(1)}, pred[6,64]{1,0:T(8,128)(4,1)}, u32[]{:S(2)}) copy-start(pred[6,64]{1,0:T(8,128)(4,1)} %copy-done.4) | copy-start | bytes 1156
  200.1 3.8 %copy-start.7 = (pred[6,128]{1,0:T(8,128)(4,1)S(1)}, pred[6,128]{1,0:T(8,128)(4,1)}, u32[]{:S(2)}) copy-start(pred[6,128]{1,0:T(8,128)(4,1)} %copy-done.6) | copy-start | bytes 2308
  200.1 3.8 %copy-start.9 = (f32[6]{0:T(128)S(1)}, f32[6]{0:T(128)}, u32[]{:S(2)}) copy-start(f32[6]{0:T(128)} %param.15) | copy-start | bytes 76
where the time goes:
time: 238 us; the launch traced here: 237 us
  blocking collectives  129 us (54%)
  matrix products  43.6 us (18%)
  local copies, waits for them, and re-layouts  25.1 us (11%)
  starting transfers between devices  19.5 us (8%)
  other arithmetic  10.4 us (4%)
  waiting for transfers between devices  6.25 us (3%)
  between operations  3.05 us (1%)
    psum x3, blocking collectives, per_device(): squares = lax.psum(jnp.sum(resid * resid), ('chain', 'pair', 'pno'))  99.2 us
    dot_general x3, matrix products, per_device(): jnp.einsum('pnac,pnbc->pnab', proj, intersections, preferred_element_type...  32.4 us
    gather x3, local copies, waits for them, and re-layouts, per_device(): blocks = jnp.take(window, slots, axis=0)  24 us
    ppermute x3, starting transfers between devices, padded(): lax.ppermute(tail, axis, [(i, (i + 1) % count) for i in range(ends)])  15.7 us
    all_gather x2, blocking collectives, spread_delta(): lax.all_gather(whole_rows.astype(jnp.bfloat16), 'pair', axis=0, tiled=True)  15.2 us
    dot_general x3, matrix products, per_device(): coupled = jnp.einsum('pn,pnab->pab', coupling, terms)  11.2 us
    all_gather x1, blocking collectives, spread_amps(): fragment_set = lax.all_gather(whole_rows, 'pair', axis=0, tiled=True)  8.7 us
    ppermute x3, waiting for transfers between devices, padded(): lax.ppermute(tail, axis, [(i, (i + 1) % count) for i in range(ends)])  6.24 us
  transfers between devices with their start and end apart: 6, of which 1 were waited for; matrix products, arithmetic and copies ran while one was open for 1% of the time, Pallas kernels for 0%

commit v1 on v0

v1 whole, which is shorter than its diff:
```python
import functools

import jax
import jax.numpy as jnp
from jax import lax
from jax.experimental import pallas as pl
from jax.experimental.pallas import tpu as pltpu
from jax.sharding import PartitionSpec as P

ITERS = 3
MESH = pl.DeviceIdType.MESH
GROUP = 4


def remote(src, dst, send_sem, recv_sem, device):
    return pltpu.make_async_remote_copy(
        src_ref=src,
        dst_ref=dst,
        send_sem=send_sem,
        recv_sem=recv_sem,
        device_id=device,
        device_id_type=MESH,
    )


def kernel(
    nchain,
    npair,
    npno,
    cells,
    nb_ref,
    coupling_ref,
    shift_ref,
    ranks_ref,
    amps_ref,
    ints_ref,
    energy_ref,
    inter_hbm,
    out_ref,
    norms_ref,
    s_vm,
    scat,
    win,
    moved,
    part,
    half_in,
    denom,
    own,
    delta,
    sums,
    load_sem,
    x_send,
    x_recv,
    p_send,
    p_recv,
    r_send,
    r_recv,
):
    z = lax.axis_index("chain")
    x = lax.axis_index("pair")
    c = lax.axis_index("pno")
    count, half, width = amps_ref.shape
    near = nb_ref.shape[1]
    total = nchain * npair * npno
    me = (z * npair + x) * npno + c
    frag = count * npair
    own_base = frag + x * count
    row0 = pl.multiple_of(c * half, half)
    row1 = pl.multiple_of((1 - c) * half, half)
    other = {"pno": 1 - c}

    loads = [pltpu.make_async_copy(inter_hbm.at[p], s_vm.at[p], load_sem.at[p]) for p in range(count)]
    for load in loads:
        load.start()

    arrive = [moved.at[t] for t in range(ITERS - 1)]
    stages = [win] + arrive

    def peer_of(j):
        peer = lax.rem(me + j, total)
        return {
            "chain": peer // (npair * npno),
            "pair": lax.rem(peer // npno, npair),
            "pno": lax.rem(peer, npno),
        }

    barrier = pltpu.get_barrier_semaphore()

    @pl.loop(1, total)
    def _(j):
        pl.semaphore_signal(barrier, inc=1, device_id=peer_of(j), device_id_type=MESH)

    rows = row0 + lax.broadcasted_iota(jnp.int32, (half, width), 0)
    cols = lax.broadcasted_iota(jnp.int32, (half, width), 1)

    def live(p):
        rank = ranks_ref[p]
        return (rows < rank) & (cols < rank)

    for p in range(count):
        mine = jnp.where(live(p), amps_ref[p].astype(jnp.float32), 0.0)
        own[p] = mine
        win[own_base + p] = mine.astype(jnp.bfloat16)

    @pl.when(z == 0)
    def _():
        for ref in stages:
            ref[pl.ds(0, frag)] = jnp.zeros((frag, half, width), jnp.bfloat16)

    @pl.when(z == nchain - 1)
    def _():
        for ref in stages:
            ref[pl.ds(2 * frag, frag)] = jnp.zeros((frag, half, width), jnp.bfloat16)

    pl.semaphore_wait(barrier, total - 1)

    partners = [
        (dz, dx) for dx in range(npair - 1, -1, -1) for dz in (-1, 1, 0) if (dz, dx) != (0, 0)
    ]

    def each_partner(act):
        for dz, dx in partners:
            if dz == 0:
                act(dz, dx)
            else:
                inside = (z > 0) if dz < 0 else (z < nchain - 1)
                pl.when(inside)(functools.partial(act, dz, dx))

    def push(t, first, size):
        def act(dz, dx):
            target = {"chain": z + dz, "pair": lax.rem(x + dx, npair)}
            dst = (1 - dz) * frag + x * count + first
            remote(
                stages[t].at[pl.ds(own_base + first, size)],
                stages[t].at[pl.ds(dst, size)],
                x_send.at[t, dz + 1, dx],
                x_recv.at[t, 1 - dz, dx],
                target,
            ).start()

        each_partner(act)

    def settle(t):
        def act(dz, dx):
            target = {"chain": z + dz, "pair": lax.rem(x + dx, npair)}
            sx = (npair - dx) % npair
            src = (1 + dz) * frag + lax.rem(x + dx, npair) * count
            copy = remote(
                stages[t].at[pl.ds(own_base, count)],
                stages[t].at[pl.ds(src, count)],
                x_send.at[t, dz + 1, dx],
                x_recv.at[t, dz + 1, sx],
                target,
            )
            copy.wait_send()
            copy.wait_recv()

        each_partner(act)

    push(0, 0, count)

    for p in range(count):
        e = energy_ref[pl.ds(p, 1), :]
        down = jnp.transpose(jnp.broadcast_to(e, (width, width)))
        part[0, p] = down
        denom[p] = part[0, p, pl.ds(row0, half), :] + e - shift_ref[p]

    for p in range(count):
        loads[p].wait()

    def pack(start):
        @pl.loop(0, count)
        def _(p):
            for k in range(near // 2):
                first = s_vm[p, 2 * k][:, start : start + half]
                second = s_vm[p, 2 * k + 1][:, start : start + half]
                scat[p, k] = jnp.concatenate([first, second], axis=1)

    for core in range(npno):
        pl.when(c == core)(functools.partial(pack, core * half))

    settle(0)
    base = (z - 1) * frag

    def partial_sum(t, p):
        acc = jnp.zeros((width, width), jnp.float32)
        for g in range(near // GROUP):
            qs = []
            for n in range(g * GROUP, (g + 1) * GROUP):
                block = win[jnp.clip(nb_ref[p, n] - base, 0, 3 * frag - 1)]
                q = lax.dot_general(
                    block,
                    s_vm[p, n],
                    (((1,), (1,)), ((), ())),
                    preferred_element_type=jnp.float32,
                )
                qs.append((q * coupling_ref[p, n]).astype(jnp.bfloat16))
            lhs = jnp.concatenate(
                [scat[p, k] for k in range(g * GROUP // 2, (g + 1) * GROUP // 2)], axis=1
            )
            acc += jnp.dot(lhs, jnp.concatenate(qs, axis=0), preferred_element_type=jnp.float32)
        part[t, p] = acc

    def swap(t, p):
        return remote(
            part.at[t, p, pl.ds(row1, half)],
            half_in.at[t, p],
            p_send.at[t, p],
            p_recv.at[t, p],
            other,
        )

    def finish(t, p, squares):
        swap(t, p).wait_recv()
        coupled = part[t, p, pl.ds(row0, half), :] + half_in[t, p]
        d = denom[p]
        resid = jnp.where(live(p), ints_ref[p].astype(jnp.float32) + coupled - d * own[p], 0.0)
        step = resid / d
        delta[p] = step
        if t + 1 < ITERS:
            arrive[t][own_base + p] = step.astype(jnp.bfloat16)
            push(t + 1, p, 1)
        return squares + jnp.sum((resid * resid).reshape(half // 8, 8, width), axis=0)

    for t in range(ITERS):
        partial_sum(t, 0)
        swap(t, 0).start()

        def body(p, squares):
            partial_sum(t, p)
            swap(t, p).start()
            return finish(t, p - 1, squares)

        squares = lax.fori_loop(1, count, body, jnp.zeros((8, width), jnp.float32))
        squares = finish(t, count - 1, squares)
        sums[t, me] = squares

        @pl.loop(1, total)
        def _(j):
            remote(sums.at[t, me], sums.at[t, me], r_send.at[t], r_recv.at[t], peer_of(j)).start()

        for p in range(count):
            swap(t, p).wait_send()
        everyone = remote(
            sums.at[t, pl.ds(0, total - 1)],
            sums.at[t, pl.ds(0, total - 1)],
            r_send.at[t],
            r_recv.at[t],
            other,
        )
        everyone.wait_send()
        everyone.wait_recv()
        squares = jnp.sum(jnp.sum(sums[t], axis=0))
        rms = jnp.sqrt(jnp.full((8, width), squares, jnp.float32) / cells)
        norms_ref[t] = rms
        factor = 1.0 / (1.0 + rms[0:1, :])
        more = t + 1 < ITERS
        for p in range(count):
            fresh = (own[p] + delta[p] * factor).astype(jnp.bfloat16)
            if more:
                own[p] = fresh.astype(jnp.float32)
            else:
                out_ref[p] = fresh
        if more:
            settle(t + 1)

            @pl.loop(0, 3 * npair)
            def _(k):
                for i in range(count):
                    at = k * count + i
                    change = arrive[t][at].astype(jnp.float32) * factor
                    win[at] = (win[at].astype(jnp.float32) + change).astype(jnp.bfloat16)


def per_device(
    amplitudes, integrals, intersections, coupling, pno_energies, pair_shift, ranks, neighbours
):
    nchain, npair, npno = (lax.axis_size(a) for a in ("chain", "pair", "pno"))
    count, half, width = amplitudes.shape
    near = neighbours.shape[1]
    frag = count * npair
    total = nchain * npair * npno
    cells = frag * nchain * width * width
    vmem = pl.BlockSpec(memory_space=pltpu.VMEM)
    smem = pl.BlockSpec(memory_space=pltpu.SMEM)
    dma = pltpu.SemaphoreType.DMA
    out, norms = pl.pallas_call(
        functools.partial(kernel, nchain, npair, npno, cells),
        out_shape=(
            jax.ShapeDtypeStruct((count, half, width), jnp.bfloat16),
            jax.ShapeDtypeStruct((ITERS, 8, width), jnp.float32),
        ),
        in_specs=[smem, smem, smem, smem, vmem, vmem, vmem, pl.BlockSpec(memory_space=pl.ANY)],
        out_specs=(vmem, vmem),
        scratch_shapes=[
            pltpu.VMEM((count, near, width, width), jnp.bfloat16),
            pltpu.VMEM((count, near // 2, width, width), jnp.bfloat16),
            pltpu.VMEM((3 * frag, half, width), jnp.bfloat16),
            pltpu.VMEM((ITERS - 1, 3 * frag, half, width), jnp.bfloat16),
            pltpu.VMEM((ITERS, count, width, width), jnp.float32),
            pltpu.VMEM((ITERS, count, half, width), jnp.float32),
            pltpu.VMEM((count, half, width), jnp.float32),
            pltpu.VMEM((count, half, width), jnp.float32),
            pltpu.VMEM((count, half, width), jnp.float32),
            pltpu.VMEM((ITERS, total, 8, width), jnp.float32),
            dma((count,)),
            dma((ITERS, 3, npair)),
            dma((ITERS, 3, npair)),
            dma((ITERS, count)),
            dma((ITERS, count)),
            dma((ITERS,)),
            dma((ITERS,)),
        ],
        compiler_params=pltpu.CompilerParams(
            collective_id=0, has_side_effects=True, vmem_limit_bytes=56 * 1024 * 1024
        ),
    )(
        neighbours,
        coupling,
        pair_shift,
        ranks,
        amplitudes,
        integrals,
        pno_energies,
        intersections,
    )
    return out, norms[:, 0, 0]


def solution(mesh):
    lead = ("job", "chain", "pair")
    in_specs = (
        P(lead, "pno", None),
        P(lead, "pno", None),
        P(lead, None, None, None),
        P(lead, None),
        P(lead, None),
        P(lead),
        P(lead),
        P(lead, None),
    )
    out_specs = (P(lead, "pno", None), P("job"))
    return jax.shard_map(
        per_device, mesh=mesh, in_specs=in_specs, out_specs=out_specs, check_vma=False
    )
```

time: 238 us -> 67.6 us (0.28)
  blocking collectives: 129 us -> 0 us
  Pallas kernels: 0 us -> 63.9 us
  matrix products: 43.6 us -> 0 us
  local copies, waits for them, and re-layouts: 25.1 us -> 2.86 us
  starting transfers between devices: 19.5 us -> 0 us
  other arithmetic: 10.4 us -> 0 us
  waiting for transfers between devices: 6.25 us -> 0 us
  between operations: 3.05 us -> 0.64 us
    psum x3 -> x0, blocking collectives: 99.2 us -> none  [per_device(): squares = lax.psum(jnp.sum(resid * resid), ('chain', 'pair', 'pno'))]
    pallas_call x0 -> x1, Pallas kernels: none -> 63.9 us  [per_device(): pl.pallas_call(functools.partial(kernel, nchain, npair, npno, cells), out...]
    dot_general x6 -> x0, matrix products: 43.6 us -> none  [the longest x3 32.4 us: per_device(): jnp.einsum('pnac,pnbc->pnab', proj, intersections, preferred_element_type...]
    all_gather x6 -> x0, blocking collectives: 29.9 us -> none  [the longest x2 15.2 us: spread_delta(): lax.all_gather(whole_rows.astype(jnp.bfloat16), 'pair', axis=0, tiled=True)]
    gather x3 -> x0, local copies, waits for them, and re-layouts: 24 us -> none  [per_device(): blocks = jnp.take(window, slots, axis=0)]
    ppermute x6 -> x0, starting transfers between devices: 19.5 us -> none  [the longest x3 15.7 us: padded(): lax.ppermute(tail, axis, [(i, (i + 1) % count) for i in range(ends)])]
    ppermute x6 -> x0, waiting for transfers between devices: 6.25 us -> none  [the longest x3 6.24 us: padded(): lax.ppermute(tail, axis, [(i, (i + 1) % count) for i in range(ends)])]
    convert_element_type x5 -> x0, other arithmetic: 5.19 us -> none  [the longest x2 3.12 us: per_device(): window = (window.astype(jnp.float32) + moved * factor).astype(jnp.bfloat16)]
  transfers between devices with their start and end apart: 6 -> 0, of which waited for: 1 -> 0; matrix products, arithmetic and copies ran while one was open for 1% -> 0% of each run, Pallas kernels for 0% -> 0%
where the time goes in v1:
time: 67.6 us; the launch traced here: 67.4 us
  Pallas kernels  63.9 us (95%)
  local copies, waits for them, and re-layouts  2.86 us (4%)
    pallas_call x1, Pallas kernels, per_device(): pl.pallas_call(functools.partial(kernel, nchain, npair, npno, cells), out...  63.9 us
    unnamed x1, local copies, waits for them, and re-layouts  1.54 us

profile of v1, /device:TPU:0, one launch (start us, length us, event | category | flops | bytes accessed | tf_op | source)
XLA Modules:
  0.0 67.4 jit_solution(3520532803356586962)
XLA Ops:
  0.6 63.9 %shard_map.95 = (bf16[6,64,128]{2,1,0:T(8,128)(2,1)}, f32[3,8,128]{2,1,0:T(8,128)}) custom-call(s32[6,32]{1,0:T(8,128)} %nb_ref.1, f32[6,32]{1,0:T(8,128)} %coupling_ref.1, f32[6]{0:T(128)} %shift_ref.1, s32[6]{0:T(128)} %ranks_ref.1, bf16[6,64,128]{2,1,0:T(8,128)(2,1)} %amps_ref.1, bf16[6,64,128]{2,1,0:T(8,128)(2,1)} %ints_ref.1, f32[6,128]{1,0:T(8,128)} %energy_ref.1, ...), custom_call_target="tpu_custom_call" | custom-call | tf_op jit(solution)/shard_map/pallas_call | solution.py:287
  64.5 1.3 %slice_reduce_fusion = f32[3]{0:T(128)} fusion(f32[3,8,128]{2,1,0:T(8,128)} %get-tuple-element.5), kind=kLoop, calls=%fused_computation | loop fusion | bytes 24 | tf_op jit(solution)/shard_map/slice | solution.py:327
  65.8 1.5 %copy.11 = bf16[6,64,128]{2,1,0:T(8,128)(2,1)} copy(bf16[6,64,128]{2,1,0:T(8,128)(2,1)} %get-tuple-element.8) | data formatting | bytes 196608

commit v2 on v1

--- a/solution.py
+++ b/solution.py
@@ -40,13 +40,14 @@
     norms_ref,
     s_vm,
     scat,
-    win,
-    moved,
+    stages,
     part,
     half_in,
     denom,
     own,
     delta,
+    csum,
+    factor,
     sums,
     load_sem,
     x_send,
@@ -73,8 +74,7 @@
     for load in loads:
         load.start()
 
-    arrive = [moved.at[t] for t in range(ITERS - 1)]
-    stages = [win] + arrive
+    win, arrive = stages[0], stages[1:]
 
     def peer_of(j):
         peer = lax.rem(me + j, total)
@@ -183,11 +183,12 @@
     base = (z - 1) * frag
 
     def partial_sum(t, p):
+        source = stages[t]
         acc = jnp.zeros((width, width), jnp.float32)
         for g in range(near // GROUP):
             qs = []
             for n in range(g * GROUP, (g + 1) * GROUP):
-                block = win[jnp.clip(nb_ref[p, n] - base, 0, 3 * frag - 1)]
+                block = source[jnp.clip(nb_ref[p, n] - base, 0, 3 * frag - 1)]
                 q = lax.dot_general(
                     block,
                     s_vm[p, n],
@@ -213,8 +214,14 @@
     def finish(t, p, squares):
         swap(t, p).wait_recv()
         coupled = part[t, p, pl.ds(row0, half), :] + half_in[t, p]
+        mine = own[p]
+        if t > 0:
+            coupled = csum[p] + factor[0:1, :] * coupled
+            mine = (mine + delta[p] * factor[0:1, :]).astype(jnp.bfloat16).astype(jnp.float32)
+            own[p] = mine
+        csum[p] = coupled
         d = denom[p]
-        resid = jnp.where(live(p), ints_ref[p].astype(jnp.float32) + coupled - d * own[p], 0.0)
+        resid = jnp.where(live(p), ints_ref[p].astype(jnp.float32) + coupled - d * mine, 0.0)
         step = resid / d
         delta[p] = step
         if t + 1 < ITERS:
@@ -222,25 +229,7 @@
             push(t + 1, p, 1)
         return squares + jnp.sum((resid * resid).reshape(half // 8, 8, width), axis=0)
 
-    for t in range(ITERS):
-        partial_sum(t, 0)
-        swap(t, 0).start()
-
-        def body(p, squares):
-            partial_sum(t, p)
-            swap(t, p).start()
-            return finish(t, p - 1, squares)
-
-        squares = lax.fori_loop(1, count, body, jnp.zeros((8, width), jnp.float32))
-        squares = finish(t, count - 1, squares)
-        sums[t, me] = squares
-
-        @pl.loop(1, total)
-        def _(j):
-            remote(sums.at[t, me], sums.at[t, me], r_send.at[t], r_recv.at[t], peer_of(j)).start()
-
-        for p in range(count):
-            swap(t, p).wait_send()
+    def absorb(t):
         everyone = remote(
             sums.at[t, pl.ds(0, total - 1)],
             sums.at[t, pl.ds(0, total - 1)],
@@ -253,23 +242,35 @@
         squares = jnp.sum(jnp.sum(sums[t], axis=0))
         rms = jnp.sqrt(jnp.full((8, width), squares, jnp.float32) / cells)
         norms_ref[t] = rms
-        factor = 1.0 / (1.0 + rms[0:1, :])
-        more = t + 1 < ITERS
+        factor[...] = 1.0 / (1.0 + rms)
+
+    for t in range(ITERS):
+        partial_sum(t, 0)
+        swap(t, 0).start()
+
+        def body(p, squares):
+            partial_sum(t, p)
+            swap(t, p).start()
+            if t > 0:
+                pl.when(p == 1)(functools.partial(absorb, t - 1))
+            return finish(t, p - 1, squares)
+
+        squares = lax.fori_loop(1, count, body, jnp.zeros((8, width), jnp.float32))
+        squares = finish(t, count - 1, squares)
+        sums[t, me] = squares
+
+        @pl.loop(1, total)
+        def _(j):
+            remote(sums.at[t, me], sums.at[t, me], r_send.at[t], r_recv.at[t], peer_of(j)).start()
+
         for p in range(count):
-            fresh = (own[p] + delta[p] * factor).astype(jnp.bfloat16)
-            if more:
-                own[p] = fresh.astype(jnp.float32)
-            else:
-                out_ref[p] = fresh
-        if more:
+            swap(t, p).wait_send()
+        if t + 1 < ITERS:
             settle(t + 1)
 
-            @pl.loop(0, 3 * npair)
-            def _(k):
-                for i in range(count):
-                    at = k * count + i
-                    change = arrive[t][at].astype(jnp.float32) * factor
-                    win[at] = (win[at].astype(jnp.float32) + change).astype(jnp.bfloat16)
+    absorb(ITERS - 1)
+    for p in range(count):
+        out_ref[p] = (own[p] + delta[p] * factor[0:1, :]).astype(jnp.bfloat16)
 
 
 def per_device(
@@ -295,13 +296,14 @@
         scratch_shapes=[
             pltpu.VMEM((count, near, width, width), jnp.bfloat16),
             pltpu.VMEM((count, near // 2, width, width), jnp.bfloat16),
-            pltpu.VMEM((3 * frag, half, width), jnp.bfloat16),
-            pltpu.VMEM((ITERS - 1, 3 * frag, half, width), jnp.bfloat16),
+            [pltpu.VMEM((3 * frag, half, width), jnp.bfloat16) for _ in range(ITERS)],
             pltpu.VMEM((ITERS, count, width, width), jnp.float32),
             pltpu.VMEM((ITERS, count, half, width), jnp.float32),
             pltpu.VMEM((count, half, width), jnp.float32),
             pltpu.VMEM((count, half, width), jnp.float32),
             pltpu.VMEM((count, half, width), jnp.float32),
+            pltpu.VMEM((count, half, width), jnp.float32),
+            pltpu.VMEM((8, width), jnp.float32),
             pltpu.VMEM((ITERS, total, 8, width), jnp.float32),
             dma((count,)),
             dma((ITERS, 3, npair)),

time: 67.6 us -> 64.4 us (0.953)
  Pallas kernels: 63.9 us -> 60.7 us
    pallas_call x1, Pallas kernels: 63.9 us -> 60.7 us  [per_device(): pl.pallas_call(functools.partial(kernel, nchain, npair, npno, cells), out...]
where the time goes in v2:
time: 64.4 us; the launch traced here: 64.2 us
  Pallas kernels  60.7 us (94%)
  local copies, waits for them, and re-layouts  2.86 us (4%)
    pallas_call x1, Pallas kernels, per_device(): pl.pallas_call(functools.partial(kernel, nchain, npair, npno, cells), out...  60.7 us
    unnamed x1, local copies, waits for them, and re-layouts  1.54 us
    slice x1, local copies, waits for them, and re-layouts, per_device(): return (out, norms[:, 0, 0])  1.32 us

profile of v2, /device:TPU:0, one launch (start us, length us, event | category | flops | bytes accessed | tf_op | source)
XLA Modules:
  0.0 64.2 jit_solution(13064401728240662706)
XLA Ops:
  0.6 60.7 %shard_map.95 = (bf16[6,64,128]{2,1,0:T(8,128)(2,1)}, f32[3,8,128]{2,1,0:T(8,128)}) custom-call(s32[6,32]{1,0:T(8,128)} %nb_ref.1, f32[6,32]{1,0:T(8,128)} %coupling_ref.1, f32[6]{0:T(128)} %shift_ref.1, s32[6]{0:T(128)} %ranks_ref.1, bf16[6,64,128]{2,1,0:T(8,128)(2,1)} %amps_ref.1, bf16[6,64,128]{2,1,0:T(8,128)(2,1)} %ints_ref.1, f32[6,128]{1,0:T(8,128)} %energy_ref.1, ...), custom_call_target="tpu_custom_call" | custom-call | tf_op jit(solution)/shard_map/pallas_call | solution.py:288
  61.3 1.3 %slice_reduce_fusion = f32[3]{0:T(128)} fusion(f32[3,8,128]{2,1,0:T(8,128)} %get-tuple-element.5), kind=kLoop, calls=%fused_computation | loop fusion | bytes 24 | tf_op jit(solution)/shard_map/slice | solution.py:329
  62.6 1.5 %copy.11 = bf16[6,64,128]{2,1,0:T(8,128)(2,1)} copy(bf16[6,64,128]{2,1,0:T(8,128)(2,1)} %get-tuple-element.8) | data formatting | bytes 196608

commit v3 on v2

--- a/solution.py
+++ b/solution.py
@@ -9,7 +9,7 @@
 
 ITERS = 3
 MESH = pl.DeviceIdType.MESH
-GROUP = 4
+GROUP = 16
 
 
 def remote(src, dst, send_sem, recv_sem, device):

time: 64.4 us -> 54.4 us (0.84)
  Pallas kernels: 60.7 us -> 50.7 us
    pallas_call x1, Pallas kernels: 60.7 us -> 50.7 us  [per_device(): pl.pallas_call(functools.partial(kernel, nchain, npair, npno, cells), out...]
where the time goes in v3:
time: 54.4 us; the launch traced here: 54.2 us
  Pallas kernels  50.7 us (93%)
  local copies, waits for them, and re-layouts  2.86 us (5%)
  between operations  0.64 us (1%)
    pallas_call x1, Pallas kernels, per_device(): pl.pallas_call(functools.partial(kernel, nchain, npair, npno, cells), out...  50.7 us
    unnamed x1, local copies, waits for them, and re-layouts  1.54 us
    slice x1, local copies, waits for them, and re-layouts, per_device(): return (out, norms[:, 0, 0])  1.32 us

profile of v3, /device:TPU:0, one launch (start us, length us, event | category | flops | bytes accessed | tf_op | source)
XLA Modules:
  0.0 54.2 jit_solution(10370127656457784833)
XLA Ops:
  0.6 50.7 %shard_map.95 = (bf16[6,64,128]{2,1,0:T(8,128)(2,1)}, f32[3,8,128]{2,1,0:T(8,128)}) custom-call(s32[6,32]{1,0:T(8,128)} %nb_ref.1, f32[6,32]{1,0:T(8,128)} %coupling_ref.1, f32[6]{0:T(128)} %shift_ref.1, s32[6]{0:T(128)} %ranks_ref.1, bf16[6,64,128]{2,1,0:T(8,128)(2,1)} %amps_ref.1, bf16[6,64,128]{2,1,0:T(8,128)(2,1)} %ints_ref.1, f32[6,128]{1,0:T(8,128)} %energy_ref.1, ...), custom_call_target="tpu_custom_call" | custom-call | tf_op jit(solution)/shard_map/pallas_call | solution.py:288
  51.3 1.3 %slice_reduce_fusion = f32[3]{0:T(128)} fusion(f32[3,8,128]{2,1,0:T(8,128)} %get-tuple-element.5), kind=kLoop, calls=%fused_computation | loop fusion | bytes 24 | tf_op jit(solution)/shard_map/slice | solution.py:329
  52.6 1.5 %copy.11 = bf16[6,64,128]{2,1,0:T(8,128)(2,1)} copy(bf16[6,64,128]{2,1,0:T(8,128)(2,1)} %get-tuple-element.8) | data formatting | bytes 196608
